TPU v7x, 32 devices: a whole 2x2x4 slice. The times are simulated.
32 devices in a mesh: dp: 8 (over y, x, core), seq: 4 (over z).
Axes of the slice: x: 2, y: 2, z: 4, core: 2. Of those that a mesh axis runs over, the one named last changes fastest.
Arguments:
- tokens: bfloat16 [8, 512, 6, 768], P('dp', 'seq'), may hold values from -6 to 6
- kind: int32 [8], P('dp'), may hold values from 0 to 1, as said below
- ln1_gain: float32 [768], replicated, may hold values from 0.1 to 1.9
- w_in: bfloat16 [768, 2304], replicated, may hold values from -0.21875 to 0.21875
- short_taps: float32 [3, 2304], replicated, may hold values from -3 to 3
- cond_taps: float32 [3, 768], replicated, may hold values from -3 to 3
- w_cond: bfloat16 [768, 768], replicated, may hold values from -0.21875 to 0.21875
- cond_bias: float32 [768], replicated, may hold values from -3 to 3
- w_out: bfloat16 [768, 768], replicated, may hold values from -0.21875 to 0.21875
- ln2_gain: float32 [768], replicated, may hold values from 0.1 to 1.9
- w_gate: bfloat16 [768, 3072], replicated, may hold values from -0.21875 to 0.21875
- w_up: bfloat16 [768, 3072], replicated, may hold values from -0.21875 to 0.21875
- w_down: bfloat16 [3072, 768], replicated, may hold values from -0.109375 to 0.109375
- cotangent: bfloat16 [8, 512, 6, 768], P('dp', 'seq'), may hold values from -6 to 6
Outputs:
- layer_out: bfloat16 [8, 512, 6, 768], P('dp', 'seq')
- grad_tokens: bfloat16 [8, 512, 6, 768], P('dp', 'seq')
- grad_ln1: float32 [768], P('seq')
- grad_w_in: float32 [768, 2304], P('seq')
- grad_short_taps: float32 [3, 2304], P(None, 'seq')
- grad_cond_taps: float32 [3, 768], P(None, 'seq')
- grad_w_cond: float32 [768, 768], P('seq')
- grad_cond_bias: float32 [768], P('seq')
- grad_w_out: float32 [768, 768], P('seq')
- grad_ln2: float32 [768], P('seq')
- grad_gate: float32 [768, 3072], P('seq')
- grad_up: float32 [768, 3072], P('seq')
- grad_down: float32 [3072, 768], P('seq')
Inputs may be any that keep to these rules, and one draw needn't show every extreme that they name: Exactly 4 groups have kind 1.
All inputs are finite; a program needn't handle non-finite values.
Results may differ from a plain program's by a relative error of at most 0.017.
Values may be sent and summed in bfloat16 or wider, within the bound.
A program may use at most 256 MiB of HBM per device.

v0:
```python
import math
import jax
import jax.numpy as jnp
from jax import lax
from jax.sharding import PartitionSpec as P

highest = lax.Precision.HIGHEST
epsilon = 1e-05


def from_behind(value, axis, by):
    peers = lax.axis_size(axis)
    pairs = [(i, i + by) for i in range(peers) if 0 <= i + by < peers]
    return lax.ppermute(value, axis, pairs)


def norm_rows(values, scale_gain):
    row_mean = jnp.mean(values, axis=-1, keepdims=True)
    centered = values - row_mean
    scale_inv = lax.rsqrt(jnp.mean(centered * centered, axis=-1, keepdims=True) + epsilon)
    normed = centered * scale_inv
    return (normed * scale_gain, normed, scale_inv)


def norm_back(grad_out, normed, scale_inv, scale_gain):
    grad_gain = jnp.sum(grad_out * normed, axis=0)
    grad_normed = grad_out * scale_gain
    inner_mean = jnp.mean(grad_normed, axis=-1, keepdims=True)
    inner_cross = jnp.mean(grad_normed * normed, axis=-1, keepdims=True)
    return (scale_inv * (grad_normed - inner_mean - normed * inner_cross), grad_gain)


def wave_tables(freq_ids, time_ids, span_len):
    fold_freq = freq_ids[:, None] % span_len
    fold_time = time_ids[None, :] % span_len
    same_block = (freq_ids[:, None] // span_len == time_ids[None, :] // span_len).astype(
        jnp.float32
    )
    phase_index = fold_freq * fold_time % span_len
    phase_angle = phase_index.astype(jnp.float32) * (2.0 * math.pi) / span_len.astype(jnp.float32)
    return (jnp.cos(phase_angle) * same_block, jnp.sin(phase_angle) * same_block)


def conv_forward(extended, taps):
    return taps[0] * extended[2:] + taps[1] * extended[1:-1] + taps[2] * extended[:-2]


def conv_backward(grad_out, extended, taps, long_flag):
    count_rows = grad_out.shape[0]
    zero_pad = jnp.zeros((2,) + grad_out.shape[1:], jnp.float32)
    padded = jnp.concatenate([grad_out, zero_pad], axis=0)
    grad_local = (
        taps[0] * padded[:count_rows] + taps[1] * padded[1 : count_rows + 1] + taps[2] * padded[2:]
    )
    grad_rim = (
        jnp.stack([taps[2] * grad_out[0], taps[1] * grad_out[0] + taps[2] * grad_out[1]])
        * long_flag
    )
    grad_taps = jnp.stack(
        [
            jnp.sum(grad_out * extended[2:], axis=(0, 1)),
            jnp.sum(grad_out * extended[1:-1], axis=(0, 1)),
            jnp.sum(grad_out * extended[:-2], axis=(0, 1)),
        ]
    )
    return (grad_local, grad_rim, grad_taps)


def on_device(
    tokens,
    kind,
    ln1_gain,
    w_in,
    short_taps,
    cond_taps,
    w_cond,
    cond_bias,
    w_out,
    ln2_gain,
    w_gate,
    w_up,
    w_down,
    cotangent,
):
    piece_rows = tokens.shape[1]
    slot_count = tokens.shape[2]
    model_width = tokens.shape[3]
    flat_rows = piece_rows * slot_count
    seq_count = lax.axis_size("seq")
    seq_rank = lax.axis_index("seq")
    is_long = kind[0]
    long_flag = is_long.astype(jnp.float32)
    span_len = jnp.where(is_long == 1, piece_rows * seq_count, piece_rows).astype(jnp.int32)
    span_float = span_len.astype(jnp.float32)
    freq_ids = seq_rank * piece_rows + jnp.arange(piece_rows, dtype=jnp.int32)
    token_rows = tokens.reshape(flat_rows, model_width).astype(jnp.float32)
    normed_one, unit_one, inv_one = norm_rows(token_rows, ln1_gain)
    normed_one_low = normed_one.astype(jnp.bfloat16)
    projected = jnp.dot(normed_one_low, w_in, preferred_element_type=jnp.float32)
    proj_low = projected.astype(jnp.bfloat16).reshape(piece_rows, slot_count, 3 * model_width)
    proj_f = proj_low.astype(jnp.float32)
    rim_proj = from_behind(proj_low[piece_rows - 2 :], "seq", 1).astype(jnp.float32) * long_flag
    extended_proj = jnp.concatenate([rim_proj, proj_f], axis=0)
    conv_out = conv_forward(extended_proj, short_taps)
    query_conv = conv_out[:, :, :model_width]
    key_conv = conv_out[:, :, model_width : 2 * model_width]
    value_low = conv_out[:, :, 2 * model_width :].astype(jnp.bfloat16)
    value_f = value_low.astype(jnp.float32)
    rim_value = from_behind(value_low[piece_rows - 2 :], "seq", 1).astype(jnp.float32) * long_flag
    extended_value = jnp.concatenate([rim_value, value_f], axis=0)
    cond_low = conv_forward(extended_value, cond_taps).astype(jnp.bfloat16)
    signal_low = (key_conv * value_f).astype(jnp.bfloat16)
    sig_piece = lax.all_gather(signal_low, "seq", axis=0, tiled=True).astype(jnp.float32)
    cond_piece = lax.all_gather(cond_low, "seq", axis=0, tiled=True).astype(jnp.float32)
    time_ids = jnp.arange(sig_piece.shape[0], dtype=jnp.int32)
    cos_table, sin_table = wave_tables(freq_ids, time_ids, span_len)
    sig_cos = jnp.einsum("ft,tsd->fsd", cos_table, sig_piece, precision=highest)
    sig_sin = jnp.einsum("ft,tsd->fsd", sin_table, sig_piece, precision=highest)
    cond_cos = jnp.einsum("ft,tsd->fsd", cos_table, cond_piece, precision=highest)
    cond_sin = jnp.einsum("ft,tsd->fsd", sin_table, cond_piece, precision=highest)
    power_spec = (cond_cos * cond_cos + cond_sin * cond_sin) / span_float
    features_low = jnp.log1p(power_spec).astype(jnp.bfloat16).reshape(flat_rows, model_width)
    pre_tanh = jnp.dot(features_low, w_cond, preferred_element_type=jnp.float32) + cond_bias
    tanh_value = jnp.tanh(pre_tanh).reshape(piece_rows, slot_count, model_width)
    spectral_gain = 1.0 + tanh_value
    gained_cos = spectral_gain * sig_cos
    gained_sin = spectral_gain * sig_sin
    time_ids = jnp.arange(piece_rows * lax.axis_size("seq"), dtype=jnp.int32)
    cos_table, sin_table = wave_tables(freq_ids, time_ids, span_len)
    term = jnp.einsum("ft,fsd->tsd", cos_table, gained_cos, precision=highest) + jnp.einsum(
        "ft,fsd->tsd", sin_table, gained_sin, precision=highest
    )
    filtered = lax.psum_scatter(
        (term / span_float).astype(jnp.bfloat16), "seq", scatter_dimension=0, tiled=True
    ).astype(jnp.float32)
    mixed_low = (query_conv * filtered).astype(jnp.bfloat16).reshape(flat_rows, model_width)
    hidden_one = token_rows + jnp.dot(mixed_low, w_out, preferred_element_type=jnp.float32)
    normed_two, unit_two, inv_two = norm_rows(hidden_one, ln2_gain)
    normed_two_low = normed_two.astype(jnp.bfloat16)
    gate_pre = jnp.dot(normed_two_low, w_gate, preferred_element_type=jnp.float32)
    up_proj = jnp.dot(normed_two_low, w_up, preferred_element_type=jnp.float32)
    gate_sig = jax.nn.sigmoid(gate_pre)
    gate_act = gate_pre * gate_sig
    hidden_act = (gate_act * up_proj).astype(jnp.bfloat16)
    layer_rows = hidden_one + jnp.dot(hidden_act, w_down, preferred_element_type=jnp.float32)
    layer_out = layer_rows.astype(jnp.bfloat16).reshape(tokens.shape)
    cot_rows = cotangent.reshape(flat_rows, model_width)
    grad_down = jnp.einsum("nf,nd->fd", hidden_act, cot_rows, preferred_element_type=jnp.float32)
    grad_act = jnp.einsum("nd,fd->nf", cot_rows, w_down, preferred_element_type=jnp.float32)
    grad_gate_pre = (grad_act * up_proj * gate_sig * (1.0 + gate_pre * (1.0 - gate_sig))).astype(
        jnp.bfloat16
    )
    grad_up_proj = (grad_act * gate_act).astype(jnp.bfloat16)
    grad_gate = jnp.einsum(
        "nd,nf->df", normed_two_low, grad_gate_pre, preferred_element_type=jnp.float32
    )
    grad_up = jnp.einsum(
        "nd,nf->df", normed_two_low, grad_up_proj, preferred_element_type=jnp.float32
    )
    grad_normed_two = jnp.einsum(
        "nf,df->nd", grad_gate_pre, w_gate, preferred_element_type=jnp.float32
    ) + jnp.einsum("nf,df->nd", grad_up_proj, w_up, preferred_element_type=jnp.float32)
    grad_hidden_part, grad_ln2 = norm_back(grad_normed_two, unit_two, inv_two, ln2_gain)
    grad_hidden = cot_rows.astype(jnp.float32) + grad_hidden_part
    grad_mix_low = grad_hidden.astype(jnp.bfloat16)
    grad_w_out = jnp.einsum(
        "nd,ne->de", mixed_low, grad_mix_low, preferred_element_type=jnp.float32
    )
    grad_mixed = jnp.einsum(
        "ne,de->nd", grad_mix_low, w_out, preferred_element_type=jnp.float32
    ).reshape(piece_rows, slot_count, model_width)
    grad_query = grad_mixed * filtered
    grad_filtered_low = (grad_mixed * query_conv).astype(jnp.bfloat16)
    grad_piece = lax.all_gather(grad_filtered_low, "seq", axis=0, tiled=True).astype(jnp.float32)
    time_ids = jnp.arange(grad_piece.shape[0], dtype=jnp.int32)
    cos_table, sin_table = wave_tables(freq_ids, time_ids, span_len)
    back_cos = jnp.einsum("ft,tsd->fsd", cos_table, grad_piece, precision=highest)
    back_sin = jnp.einsum("ft,tsd->fsd", sin_table, grad_piece, precision=highest)
    back_cos = back_cos / span_float
    back_sin = back_sin / span_float
    grad_gain_spec = back_cos * sig_cos + back_sin * sig_sin
    grad_sig_cos = spectral_gain * back_cos
    grad_sig_sin = spectral_gain * back_sin
    grad_pre_low = (
        (grad_gain_spec * (1.0 - tanh_value * tanh_value))
        .astype(jnp.bfloat16)
        .reshape(flat_rows, model_width)
    )
    grad_w_cond = jnp.einsum(
        "nc,nd->cd", features_low, grad_pre_low, preferred_element_type=jnp.float32
    )
    grad_cond_bias = jnp.sum(grad_pre_low.astype(jnp.float32), axis=0)
    grad_features = jnp.einsum(
        "nd,cd->nc", grad_pre_low, w_cond, preferred_element_type=jnp.float32
    ).reshape(piece_rows, slot_count, model_width)
    grad_power = grad_features / (1.0 + power_spec)
    grad_cond_cos = 2.0 * cond_cos * grad_power / span_float
    grad_cond_sin = 2.0 * cond_sin * grad_power / span_float
    time_ids = jnp.arange(piece_rows * lax.axis_size("seq"), dtype=jnp.int32)
    cos_table, sin_table = wave_tables(freq_ids, time_ids, span_len)
    signal_term = jnp.einsum(
        "ft,fsd->tsd", cos_table, grad_sig_cos, precision=highest
    ) + jnp.einsum("ft,fsd->tsd", sin_table, grad_sig_sin, precision=highest)
    cond_term = jnp.einsum("ft,fsd->tsd", cos_table, grad_cond_cos, precision=highest) + jnp.einsum(
        "ft,fsd->tsd", sin_table, grad_cond_sin, precision=highest
    )
    source_grads = lax.psum_scatter(
        jnp.concatenate([signal_term, cond_term], axis=2).astype(jnp.bfloat16),
        "seq",
        scatter_dimension=0,
        tiled=True,
    ).astype(jnp.float32)
    grad_signal = source_grads[:, :, :model_width]
    grad_cond = source_grads[:, :, model_width:]
    grad_value_cond, grad_value_rim, grad_cond_taps = conv_backward(
        grad_cond, extended_value, cond_taps, long_flag
    )
    grad_value = grad_signal * key_conv + grad_value_cond
    grad_key = grad_signal * value_f
    value_back = from_behind(grad_value_rim.astype(jnp.bfloat16), "seq", -1).astype(
        grad_value_rim.dtype
    )
    grad_value = jnp.concatenate(
        [grad_value[: piece_rows - 2], grad_value[piece_rows - 2 :] + value_back], axis=0
    )
    grad_conv = jnp.concatenate([grad_query, grad_key, grad_value], axis=2)
    grad_proj_local, grad_proj_rim, grad_short_taps = conv_backward(
        grad_conv, extended_proj, short_taps, long_flag
    )
    proj_back = from_behind(grad_proj_rim.astype(jnp.bfloat16), "seq", -1).astype(
        grad_proj_rim.dtype
    )
    grad_proj = jnp.concatenate(
        [grad_proj_local[: piece_rows - 2], grad_proj_local[piece_rows - 2 :] + proj_back], axis=0
    )
    grad_proj_low = grad_proj.astype(jnp.bfloat16).reshape(flat_rows, 3 * model_width)
    grad_w_in = jnp.einsum(
        "nd,ne->de", normed_one_low, grad_proj_low, preferred_element_type=jnp.float32
    )
    grad_normed_one = jnp.einsum(
        "ne,de->nd", grad_proj_low, w_in, preferred_element_type=jnp.float32
    )
    grad_token_part, grad_ln1 = norm_back(grad_normed_one, unit_one, inv_one, ln1_gain)
    grad_tokens = (grad_hidden + grad_token_part).astype(jnp.bfloat16).reshape(tokens.shape)
    whole_sums = lax.psum(
        (
            grad_ln1,
            grad_w_in,
            grad_short_taps,
            grad_cond_taps,
            grad_w_cond,
            grad_cond_bias,
            grad_w_out,
            grad_ln2,
            grad_gate,
            grad_up,
            grad_down,
        ),
        ("dp", "seq"),
    )
    seq_dims = (0, 0, 1, 1, 0, 0, 0, 0, 0, 0, 0)
    summed = tuple(
        (
            lax.dynamic_slice_in_dim(
                whole_sum,
                seq_rank * (whole_sum.shape[axis_dim] // seq_count),
                whole_sum.shape[axis_dim] // seq_count,
                axis_dim,
            )
            for whole_sum, axis_dim in zip(whole_sums, seq_dims)
        )
    )
    return (
        layer_out,
        grad_tokens,
        summed[0],
        summed[1],
        summed[2],
        summed[3],
        summed[4],
        summed[5],
        summed[6],
        summed[7],
        summed[8],
        summed[9],
        summed[10],
    )


def solution(mesh):
    return jax.shard_map(
        on_device,
        mesh=mesh,
        in_specs=(
            P("dp", "seq", None, None),
            P("dp"),
            P(),
            P(),
            P(),
            P(),
            P(),
            P(),
            P(),
            P(),
            P(),
            P(),
            P(),
            P("dp", "seq", None, None),
        ),
        out_specs=(
            P("dp", "seq", None, None),
            P("dp", "seq", None, None),
            P("seq"),
            P("seq", None),
            P(None, "seq"),
            P(None, "seq"),
            P("seq", None),
            P("seq"),
            P("seq", None),
            P("seq"),
            P("seq", None),
            P("seq", None),
            P("seq", None),
        ),
        check_vma=False,
    )
```

profile of v0, /device:TPU:0, one launch (start us, length us, event | category | flops | bytes accessed | tf_op | source)
XLA Modules:
  0.0 1427.0 jit_solution(9233570854723160421)
XLA Ops:
  63.7 89.3 %all-gather.4.cloned.1.call-done = bf16[512,6,768]{2,0,1:T(8,128)(2,1)} async-done(((bf16[128,6,768]{2,0,1:T(8,128)(2,1)}), bf16[512,6,768]{2,0,1:T(8,128)(2,1)}) %all-gather.4.cloned.1.call-update) | async-done | bytes 4718608 | tf_op jit(solution)/shard_map/all_gather | solution.py:114
  153.0 8.0 fusion.64
  161.0 8.2 log-plus-one_convert_fusion
  183.9 59.2 %all-gather.6.cloned.1.call-done = bf16[512,6,768]{2,0,1:T(8,128)(2,1)} async-done(((bf16[128,6,768]{2,0,1:T(8,128)(2,1)}), bf16[512,6,768]{2,0,1:T(8,128)(2,1)}) %all-gather.6.cloned.1.call-update) | async-done | bytes 4718608 | tf_op jit(solution)/shard_map/all_gather | solution.py:113
  243.1 7.8 fusion.62
  251.0 11.7 fusion.26
  269.6 14.8 %divide_convert_fusion = bf16[512,6,768]{2,0,1:T(8,128)(2,1)} fusion(f32[512,6,768]{2,0,1:T(8,128)S(1)} %fusion.26, f32[]{:T(128)S(6)} %convert_element_type.160, f32[128,6,768]{2,0,1:T(8,128)S(1)} %fusion.54, f32[128,6,768]{2,1,0:T(8,128)S(1)} %copy-done.2, s32[]{:T(128)S(6)} %select_n.103, s32[512]{0:T(512)S(1)} %get-tuple-element.107, ...), kind=kOutput, calls=%fused_computation.8 | convolution fusion | flops 3632332800 | bytes 18879496 | tf_op jit(solution)/shard_map/ft,fsd->tsd/dot_general | solution.py:130
  291.1 77.2 %reduce-scatter.3.cloned.1.call-done = bf16[128,6,768]{2,0,1:T(8,128)(2,1)} async-done(((bf16[512,6,768]{2,0,1:T(8,128)(2,1)}), bf16[128,6,768]{2,0,1:T(8,128)(2,1)}) %reduce-scatter.3.cloned.1.call-update) | async-done | bytes 1179664 | tf_op jit(solution)/shard_map/reduce_scatter | solution.py:133
  380.3 9.2 fusion.142
  395.8 17.3 %multiply_convert_fusion = (bf16[768,3072]{1,0:T(8,128)(2,1)}, bf16[768,3072]{1,0:T(8,128)(2,1)}, bf16[768,3072]{1,0:T(8,128)(2,1)}) fusion(f32[768,3072]{1,0:T(8,128)} %fusion.142, f32[768,3072]{1,0:T(8,128)} %fusion.143, bf16[768,768]{1,0:T(8,128)(2,1)S(1)} %copy-done.31, bf16[3072,768]{1,0:T(8,128)(2,1)} %param.26), kind=kOutput, calls=%fused_computation.3 | convolution fusion | flops 3659268096 | bytes 38928384 | tf_op jit(solution)/shard_map/nd,fd->nf/dot_general | solution.py:149
  413.1 7.7 fusion.144
  446.3 86.3 %all-gather.8.cloned.1.call-done = bf16[512,6,768]{2,0,1:T(8,128)(2,1)} async-done(((bf16[128,6,768]{2,0,1:T(8,128)(2,1)}), bf16[512,6,768]{2,0,1:T(8,128)(2,1)}) %all-gather.8.cloned.1.call-update) | async-done | bytes 4718608 | tf_op jit(solution)/shard_map/all_gather | solution.py:174
  532.6 7.9 convolution_divide_fusion.1
  540.6 11.6 fusion.23
  552.3 9.2 convert_reduce_fusion
  565.7 11.2 fusion.18
  577.0 15.4 %add_convert_fusion = bf16[512,6,768]{2,0,1:T(8,128)(2,1)} fusion(f32[512,6,768]{2,0,1:T(8,128)S(1)} %fusion.18, f32[128,6,768]{2,0,1:T(8,128)S(1)} %add_divide_fusion.1, f32[128,6,768]{2,0,1:T(8,128)} %get-tuple-element.101, f32[]{:T(128)S(6)} %convert_element_type.160, s32[]{:T(128)S(6)} %select_n.103, s32[512]{0:T(512)S(1)} %get-tuple-element.107, ...), kind=kOutput, calls=%fused_computation.1 | convolution fusion | flops 3631153152 | bytes 18879496 | tf_op jit(solution)/shard_map/ft,fsd->tsd/dot_general | solution.py:204
  592.3 15.3 %add_convert_fusion.1 = bf16[512,6,768]{2,0,1:T(8,128)(2,1)S(1)} fusion(f32[512,6,768]{2,0,1:T(8,128)S(1)} %fusion.23, f32[128,6,768]{2,0,1:T(8,128)} %get-tuple-element.105, f32[128,6,768]{2,1,0:T(8,128)S(1)} %copy-done.3, f32[]{:T(128)S(6)} %convert_element_type.160, s32[]{:T(128)S(6)} %select_n.103, s32[512]{0:T(512)S(1)} %get-tuple-element.107, ...), kind=kOutput, calls=%fused_computation.2 | convolution fusion | flops 3629973504 | bytes 18879496 | tf_op jit(solution)/shard_map/ft,fsd->tsd/dot_general | solution.py:203
  624.6 8.8 fusion.146
  648.8 123.1 %reduce-scatter.5.cloned.1.call-done = bf16[128,6,1536]{2,0,1:T(8,128)(2,1)} async-done(((bf16[512,6,1536]{2,0,1:T(8,128)(2,1)}), bf16[128,6,1536]{2,0,1:T(8,128)(2,1)}) %reduce-scatter.5.cloned.1.call-update) | async-done | bytes 2359312 | tf_op jit(solution)/shard_map/reduce_scatter | solution.py:207
  803.4 8.2 fusion.145
  816.6 10.0 add_convert_fusion.3
  876.4 44.4 %all-reduce.2 = (f32[768]{0:T(1024)}, f32[3,2304]{1,0:T(4,128)}, f32[3,768]{1,0:T(4,128)}, f32[768]{0:T(1024)}, f32[768]{0:T(1024)}) all-reduce(f32[768]{0:T(1024)} %get-tuple-element.58, f32[3,2304]{1,0:T(4,128)} %pad_maximum_fusion.4, f32[3,768]{1,0:T(4,128)S(1)} %copy-done.56, ...), channel_id=1, replica_groups=mesh['dp'=8,'seq'=4] {'dp','seq'}, use_global_device_ids=true, to_apply=%region_11.12 | all-reduce | flops 11520 | bytes 92160 | tf_op jit(solution)/shard_map/psum | solution.py:245
  927.5 476.0 %all-reduce.6.cloned.1.call-done = (f32[768,2304]{1,0:T(8,128)}, f32[768,768]{1,0:T(8,128)}, f32[768,768]{1,0:T(8,128)}, f32[768,3072]{1,0:T(8,128)}, f32[768,3072]{1,0:T(8,128)}, /*index=5*/f32[3072,768]{1,0:T(8,128)}) async-done(((f32[768,2304]{1,0:T(8,128)}, f32[768,768]{1,0:T(8,128)}, f32[768,768]{1,0:T(8,128)}, f32[768,3072]{1,0:T(8,128)}, f32[768,3072]{1,0:T(8,128)}, ...) | async-done | bytes 40108048 | tf_op jit(solution)/shard_map/psum | solution.py:245
  (301 shorter events, 273.0 us)
Async XLA Ops:
  7.2 11.9 copy-start
  7.2 145.8 %all-gather.4.cloned.1.call-start = ((), (), s32[]{:S(2)}) async-start(), calls=%async_computation.2 | async-start | bytes 5898240 | tf_op jit(solution)/shard_map/all_gather | solution.py:114
  30.1 22.0 %collective-permute-start = (bf16[2,6,2304]{2,0,1:T(2,128)(2,1)}, bf16[2,6,2304]{2,0,1:T(2,128)(2,1)}, u32[]{:S(2)}, u32[]{:S(2)}) collective-permute-start(bf16[2,6,2304]{2,0,1:T(2,128)(2,1)} %copy.78), channel_id=1, source_target_pairs={{0,1},{1,2},{2,3},{4,5},{5,6},{6,7},{8,9},{9,10},{10,11},{12,13},{... | collective-permute-start | bytes 165896 | tf_op jit(solution)/shard_map/ppermute | solution.py:14
  37.2 15.8 %copy-start.44 = (f32[2304]{0:T(1024)}, f32[2304]{0:T(1024)S(1)}, u32[]{:S(2)}) copy-start(f32[2304]{0:T(1024)S(1)} %get-tuple-element.64) | copy-start | bytes 27652
  38.7 21.7 %copy-start.52 = (f32[768]{0:T(1024)}, f32[768]{0:T(1024)S(1)}, u32[]{:S(2)}) copy-start(f32[768]{0:T(1024)S(1)} %get-tuple-element.67) | copy-start | bytes 9220
  55.9 4.5 collective-permute-start.1
  62.5 180.6 %all-gather.6.cloned.1.call-start = ((), (), s32[]{:S(2)}) async-start(), calls=%async_computation.3 | async-start | bytes 5898240 | tf_op jit(solution)/shard_map/all_gather | solution.py:113
  63.2 305.1 %reduce-scatter.3.cloned.1.call-start = ((), (), s32[]{:S(2)}) async-start(), calls=%async_computation.4 | async-start | bytes 5898240 | tf_op jit(solution)/shard_map/reduce_scatter | solution.py:133
  243.1 19.6 %slice-start.2 = ((s8[4718592]{0:T(1024)(128)(4,1)}), s8[4194304]{0:T(1024)(128)(4,1)S(1)}, s32[]{:S(2)}) async-start(s8[4718592]{0:T(1024)(128)(4,1)} %bitcast.76), calls=%async_computation.10 | async-start | bytes 8388608
  251.0 11.7 copy-start.7
  251.0 11.7 slice-start.3
  284.5 248.1 %all-gather.8.cloned.1.call-start = ((), (), s32[]{:S(2)}) async-start(), calls=%async_computation.5 | async-start | bytes 5898240 | tf_op jit(solution)/shard_map/all_gather | solution.py:174
  379.2 49.0 %copy-start.5 = (f32[768,768]{1,0:T(8,128)}, f32[768,768]{1,0:T(8,128)S(1)}, u32[]{:S(2)}) copy-start(f32[768,768]{1,0:T(8,128)S(1)} %get-tuple-element.103) | copy-start | bytes 7077892
  442.5 329.4 %reduce-scatter.5.cloned.1.call-start = ((), (), s32[]{:S(2)}) async-start(), calls=%async_computation.6 | async-start | bytes 11796480 | tf_op jit(solution)/shard_map/reduce_scatter | solution.py:207
  532.6 19.6 %slice-start.4 = ((s8[4718592]{0:T(1024)(128)(4,1)}), s8[4194304]{0:T(1024)(128)(4,1)S(1)}, s32[]{:S(2)}) async-start(s8[4718592]{0:T(1024)(128)(4,1)} %bitcast.78), calls=%async_computation.12 | async-start | bytes 8388608
  540.5 11.7 copy-start.8
  592.3 15.3 %copy-start.18 = (bf16[512,6,768]{2,0,1:T(8,128)(2,1)S(1)}, bf16[512,6,768]{2,0,1:T(8,128)(2,1)}, u32[]{:S(2)}) copy-start(bf16[512,6,768]{2,0,1:T(8,128)(2,1)} %add_convert_fusion) | copy-start | bytes 14155780
  612.0 791.5 %all-reduce.6.cloned.1.call-start = ((), (), s32[]{:S(2)}) async-start(), calls=%async_computation.7 | async-start | bytes 80216064 | tf_op jit(solution)/shard_map/psum | solution.py:245
  619.9 13.5 slice-start.6
  624.6 15.2 %slice-start.10 = ((s8[4718592]{0:T(1024)(128)(4,1)}), s8[4194304]{0:T(1024)(128)(4,1)S(1)}, s32[]{:S(2)}) async-start(s8[4718592]{0:T(1024)(128)(4,1)} %bitcast.84), calls=%async_computation.18 | async-start | bytes 8388608
  648.8 125.6 %copy-start.53 = (f32[768]{0:T(1024)S(1)}, f32[768]{0:T(1024)}, u32[]{:S(2)}) copy-start(f32[768]{0:T(1024)} %copy-done.52) | copy-start | bytes 9220
  648.8 125.6 %copy-start.55 = (f32[768]{0:T(1024)S(1)}, f32[768]{0:T(1024)}, u32[]{:S(2)}) copy-start(f32[768]{0:T(1024)} %get-tuple-element.68) | copy-start | bytes 9220
  774.5 5.9 collective-permute-start.2
  785.6 6.8 collective-permute-start.3
  (69 other events, 368.7 us)
Sparse Core Ops, SparseCore 0:
  62.6 90.3 all-gather.3
  155.2 87.9 all-gather.5
  284.6 83.6 reduce-scatter.2
  442.6 89.9 all-gather.7
  612.1 159.7 reduce-scatter.4
  811.8 591.6 all-reduce.5
where the time goes:
time: 1440 us; the launch traced here: 1430 us
  waiting for transfers between devices  916 us (64%)
  matrix products  246 us (17%)
  local copies, waits for them, and re-layouts  146 us (10%)
  other arithmetic  46.6 us (3%)
  blocking collectives  44.4 us (3%)
  between operations  16.2 us (1%)
    psum x1, waiting for transfers between devices, on_device(): lax.psum((grad_ln1, grad_w_in, grad_short_taps, grad_cond_taps, grad_w_co...  476 us
    reduce_scatter x1, waiting for transfers between devices, on_device(): lax.psum_scatter(jnp.concatenate([signal_term, cond_term], axis=2).astype...  123 us
    all_gather x1, waiting for transfers between devices, on_device(): lax.all_gather(cond_low, 'seq', axis=0, tiled=True).astype(jnp.float32)  89.3 us
    all_gather x1, waiting for transfers between devices, on_device(): lax.all_gather(grad_filtered_low, 'seq', axis=0, tiled=True)  86.3 us
    reduce_scatter x1, waiting for transfers between devices, on_device(): lax.psum_scatter((term / span_float).astype(jnp.bfloat16), 'seq', scatter...  77.2 us
    all_gather x1, waiting for transfers between devices, on_device(): lax.all_gather(signal_low, 'seq', axis=0, tiled=True).astype(jnp.float32)  59.2 us
    psum x1, blocking collectives, on_device(): lax.psum((grad_ln1, grad_w_in, grad_short_taps, grad_cond_taps, grad_w_co...  44.4 us
  transfers between devices with their start and end apart: 10, of which 8 were waited for; matrix products, arithmetic and copies ran while one was open for 12% of the time, Pallas kernels for 0%

commit v1 on v0

--- a/solution.py
+++ b/solution.py
@@ -243,20 +243,23 @@
     grad_token_part, grad_ln1 = norm_back(grad_normed_one, unit_one, inv_one, ln1_gain)
     grad_tokens = (grad_hidden + grad_token_part).astype(jnp.bfloat16).reshape(tokens.shape)
     whole_sums = lax.psum(
-        (
-            grad_ln1,
-            grad_w_in,
-            grad_short_taps,
-            grad_cond_taps,
-            grad_w_cond,
-            grad_cond_bias,
-            grad_w_out,
-            grad_ln2,
-            grad_gate,
-            grad_up,
-            grad_down,
+        lax.psum(
+            (
+                grad_ln1,
+                grad_w_in,
+                grad_short_taps,
+                grad_cond_taps,
+                grad_w_cond,
+                grad_cond_bias,
+                grad_w_out,
+                grad_ln2,
+                grad_gate,
+                grad_up,
+                grad_down,
+            ),
+            "seq",
         ),
-        ("dp", "seq"),
+        "dp",
     )
     seq_dims = (0, 0, 1, 1, 0, 0, 0, 0, 0, 0, 0)
     summed = tuple(

time: 1440 us -> 2650 us (1.84)
  waiting for transfers between devices: 916 us -> 2130 us
    psum x1, waiting for transfers between devices: 476 us -> 1330 us  [on_device(): lax.psum((grad_ln1, grad_w_in, grad_short_taps, grad_cond_taps, grad_w_co...]
    psum x0 -> x1, waiting for transfers between devices: none -> 364 us  [on_device(): lax.psum(lax.psum((grad_ln1, grad_w_in, grad_short_taps, grad_cond_taps,...]
  transfers between devices with their start and end apart: 10 -> 11, of which waited for: 8 -> 9; matrix products, arithmetic and copies ran while one was open for 12% -> 6% of each run, Pallas kernels for 0% -> 0%
where the time goes in v1:
time: 2650 us; the launch traced here: 2640 us
  waiting for transfers between devices  2130 us (80%)
  matrix products  245 us (9%)
  local copies, waits for them, and re-layouts  145 us (5%)
  other arithmetic  46.5 us (2%)
  blocking collectives  45.2 us (2%)
    psum x1, waiting for transfers between devices, on_device(): lax.psum((grad_ln1, grad_w_in, grad_short_taps, grad_cond_taps, grad_w_co...  1330 us
    psum x1, waiting for transfers between devices, on_device(): lax.psum(lax.psum((grad_ln1, grad_w_in, grad_short_taps, grad_cond_taps,...  364 us
    reduce_scatter x1, waiting for transfers between devices, on_device(): lax.psum_scatter(jnp.concatenate([signal_term, cond_term], axis=2).astype...  123 us
    all_gather x1, waiting for transfers between devices, on_device(): lax.all_gather(cond_low, 'seq', axis=0, tiled=True).astype(jnp.float32)  89.3 us
    all_gather x1, waiting for transfers between devices, on_device(): lax.all_gather(grad_filtered_low, 'seq', axis=0, tiled=True)  86.2 us
    reduce_scatter x1, waiting for transfers between devices, on_device(): lax.psum_scatter((term / span_float).astype(jnp.bfloat16), 'seq', scatter...  77.2 us
    all_gather x1, waiting for transfers between devices, on_device(): lax.all_gather(signal_low, 'seq', axis=0, tiled=True).astype(jnp.float32)  59.2 us
  transfers between devices with their start and end apart: 11, of which 9 were waited for; matrix products, arithmetic and copies ran while one was open for 6% of the time, Pallas kernels for 0%

profile of v1, /device:TPU:0, one launch (start us, length us, event | category | flops | bytes accessed | tf_op | source)
XLA Modules:
  0.0 2639.4 jit_solution(13894792493976377782)
XLA Ops:
  63.7 89.3 %all-gather.4.cloned.1.call-done = bf16[512,6,768]{2,0,1:T(8,128)(2,1)} async-done(((bf16[128,6,768]{2,0,1:T(8,128)(2,1)}), bf16[512,6,768]{2,0,1:T(8,128)(2,1)}) %all-gather.4.cloned.1.call-update) | async-done | bytes 4718608 | tf_op jit(solution)/shard_map/all_gather | solution.py:114
  153.0 8.0 fusion.64
  161.0 8.2 log-plus-one_convert_fusion
  183.9 59.2 %all-gather.6.cloned.1.call-done = bf16[512,6,768]{2,0,1:T(8,128)(2,1)} async-done(((bf16[128,6,768]{2,0,1:T(8,128)(2,1)}), bf16[512,6,768]{2,0,1:T(8,128)(2,1)}) %all-gather.6.cloned.1.call-update) | async-done | bytes 4718608 | tf_op jit(solution)/shard_map/all_gather | solution.py:113
  251.0 11.7 fusion.26
  269.6 14.8 divide_convert_fusion
  291.1 77.2 %reduce-scatter.3.cloned.1.call-done = bf16[128,6,768]{2,0,1:T(8,128)(2,1)} async-done(((bf16[512,6,768]{2,0,1:T(8,128)(2,1)}), bf16[128,6,768]{2,0,1:T(8,128)(2,1)}) %reduce-scatter.3.cloned.1.call-update) | async-done | bytes 1179664 | tf_op jit(solution)/shard_map/reduce_scatter | solution.py:133
  380.2 9.2 fusion.142
  395.7 17.2 multiply_convert_fusion
  446.2 86.2 %all-gather.8.cloned.1.call-done = bf16[512,6,768]{2,0,1:T(8,128)(2,1)} async-done(((bf16[128,6,768]{2,0,1:T(8,128)(2,1)}), bf16[512,6,768]{2,0,1:T(8,128)(2,1)}) %all-gather.8.cloned.1.call-update) | async-done | bytes 4718608 | tf_op jit(solution)/shard_map/all_gather | solution.py:174
  532.5 7.9 convolution_divide_fusion.1
  540.5 11.6 fusion.23
  552.2 9.2 convert_reduce_fusion
  565.7 11.2 fusion.18
  576.9 15.4 add_convert_fusion
  592.3 15.3 add_convert_fusion.1
  624.7 8.9 fusion.146
  648.8 123.1 %reduce-scatter.5.cloned.1.call-done = bf16[128,6,1536]{2,0,1:T(8,128)(2,1)} async-done(((bf16[512,6,1536]{2,0,1:T(8,128)(2,1)}), bf16[128,6,1536]{2,0,1:T(8,128)(2,1)}) %reduce-scatter.5.cloned.1.call-update) | async-done | bytes 2359312 | tf_op jit(solution)/shard_map/reduce_scatter | solution.py:207
  803.4 8.2 fusion.145
  811.6 1326.3 %all-reduce.11.cloned.1.call-done = (f32[768,2304]{1,0:T(8,128)}, f32[768,768]{1,0:T(8,128)}, f32[768,768]{1,0:T(8,128)}, f32[768,3072]{1,0:T(8,128)}, f32[768,3072]{1,0:T(8,128)}, /*index=5*/f32[3072,768]{1,0:T(8,128)}) async-done(((f32[768,2304]{1,0:T(8,128)}, f32[768,768]{1,0:T(8,128)}, f32[768,768]{1,0:T(8,128)}, f32[768,3072]{1,0:T(8,128)}, f32[768,3072]{1,0:T(8,128)}, ...) | async-done | bytes 40108048 | tf_op jit(solution)/shard_map/psum | solution.py:246
  2142.9 8.6 add_convert_fusion.3
  2201.3 19.4 all-reduce.4
  2220.7 25.9 all-reduce.2
  2251.9 364.0 %all-reduce.9.cloned.1.call-done = (f32[768,2304]{1,0:T(8,128)}, f32[768,768]{1,0:T(8,128)}, f32[768,768]{1,0:T(8,128)}, f32[768,3072]{1,0:T(8,128)}, f32[768,3072]{1,0:T(8,128)}, /*index=5*/f32[3072,768]{1,0:T(8,128)}) async-done(((f32[768,2304]{1,0:T(8,128)}, f32[768,768]{1,0:T(8,128)}, f32[768,768]{1,0:T(8,128)}, f32[768,3072]{1,0:T(8,128)}, f32[768,3072]{1,0:T(8,128)}, ...) | async-done | bytes 40108048 | tf_op jit(solution)/shard_map/psum | solution.py:245
  (305 shorter events, 287.2 us)
Async XLA Ops:
  7.2 11.9 copy-start
  7.2 145.8 %all-gather.4.cloned.1.call-start = ((), (), s32[]{:S(2)}) async-start(), calls=%async_computation.2 | async-start | bytes 5898240 | tf_op jit(solution)/shard_map/all_gather | solution.py:114
  30.1 22.0 collective-permute-start
  37.2 15.8 copy-start.44
  38.7 21.7 copy-start.52
  55.9 4.5 collective-permute-start.1
  62.5 180.6 %all-gather.6.cloned.1.call-start = ((), (), s32[]{:S(2)}) async-start(), calls=%async_computation.3 | async-start | bytes 5898240 | tf_op jit(solution)/shard_map/all_gather | solution.py:113
  63.2 305.0 %reduce-scatter.3.cloned.1.call-start = ((), (), s32[]{:S(2)}) async-start(), calls=%async_computation.4 | async-start | bytes 5898240 | tf_op jit(solution)/shard_map/reduce_scatter | solution.py:133
  243.1 19.6 slice-start.2
  251.0 11.7 copy-start.7
  251.0 11.7 slice-start.3
  284.4 248.1 %all-gather.8.cloned.1.call-start = ((), (), s32[]{:S(2)}) async-start(), calls=%async_computation.5 | async-start | bytes 5898240 | tf_op jit(solution)/shard_map/all_gather | solution.py:174
  379.1 48.9 %copy-start.5 = (f32[768,768]{1,0:T(8,128)}, f32[768,768]{1,0:T(8,128)S(1)}, u32[]{:S(2)}) copy-start(f32[768,768]{1,0:T(8,128)S(1)} %get-tuple-element.114) | copy-start | bytes 7077892
  442.4 329.5 %reduce-scatter.5.cloned.1.call-start = ((), (), s32[]{:S(2)}) async-start(), calls=%async_computation.6 | async-start | bytes 11796480 | tf_op jit(solution)/shard_map/reduce_scatter | solution.py:207
  532.5 19.6 slice-start.4
  592.3 15.3 copy-start.18
  612.0 1525.9 %all-reduce.11.cloned.1.call-start = ((), (), s32[]{:S(2)}) async-start(), calls=%async_computation.8 | async-start | bytes 80216064 | tf_op jit(solution)/shard_map/psum | solution.py:246
  619.9 13.7 slice-start.6
  624.6 15.2 slice-start.10
  648.8 125.6 %copy-start.53 = (f32[768]{0:T(1024)S(1)}, f32[768]{0:T(1024)}, u32[]{:S(2)}) copy-start(f32[768]{0:T(1024)} %copy-done.52) | copy-start | bytes 9220
  648.8 125.6 %copy-start.55 = (f32[768]{0:T(1024)S(1)}, f32[768]{0:T(1024)}, u32[]{:S(2)}) copy-start(f32[768]{0:T(1024)} %get-tuple-element.68) | copy-start | bytes 9220
  774.5 5.9 collective-permute-start.2
  785.6 6.8 collective-permute-start.3
  811.6 1804.3 %all-reduce.9.cloned.1.call-start = ((), (), s32[]{:S(2)}) async-start(), calls=%async_computation.7 | async-start | bytes 80216064 | tf_op jit(solution)/shard_map/psum | solution.py:245
  (70 other events, 379.7 us)
Sparse Core Ops, SparseCore 0:
  62.6 90.3 all-gather.3
  155.2 87.9 all-gather.5
  284.5 83.6 reduce-scatter.2
  442.5 89.9 all-gather.7
  612.1 159.7 reduce-scatter.4
  811.7 1326.1 all-reduce.10
  2142.9 472.9 all-reduce.8
